TPU v7x, 512 devices: a whole 4x8x8 slice. The times are simulated.
512 devices in a mesh: wide: 64 (over y, z_lo, core), narrow: 8 (over x, z_hi).
Axes of the slice: x: 4, y: 8, z: 8 (z_hi: 2, z_lo: 4; z = z_hi * 4 + z_lo), core: 2. Of those that a mesh axis runs over, the one named last changes fastest.
Arguments:
- loads: float32 [2048, 24, 128], P(('wide', 'narrow')), may hold values from -6 to 6
- diagonal: float32 [2048, 128], P(('wide', 'narrow')), may hold values from 2 to 7
- stiffness: float32 [2048, 4, 128, 128], P(('wide', 'narrow')), may hold values from 0 to 0.001953125
- neighbors: int32 [2048, 4], P(('wide', 'narrow')), may hold values from 0 to 7
- slot_mask: int32 [2048, 4], P(('wide', 'narrow')), may hold values 0 or 1
- send_list: int32 [2048], P(('wide', 'narrow')), may hold values from 0 to 3
- aggregate: int32 [2048, 128], P(('wide', 'narrow')), may hold values from 0 to 127
- coarse_inverse: float32 [8192, 8192], P(('wide', 'narrow')), may hold values from -0.0078125 to 0.0078125
Outputs:
- correction: float32 [2048, 24, 128], P(('wide', 'narrow'))
- residual: float32 [2048, 24, 128], P(('wide', 'narrow'))
Inputs may be any that keep to these rules, and one draw needn't show every extreme that they name: `neighbors`: indices into the extended list of the block's group. `send_list`: block indices within the sending group. aggregate indices among the 128 aggregates of the particle's wide coordinate.
All inputs are finite; a program needn't handle non-finite values. No bound on the sum of `slot_mask` on one device may be relied on, other than what follows from the above.
Results may differ from a plain program's by a relative error of at most 0.00025.
Values sent between devices are 32-bit elements; how exact they have to be, the bound alone decides.
A program may use at most 64 MiB of HBM per device.

v0:
```python
import jax
import jax.numpy as jnp
from jax import lax
from jax.sharding import PartitionSpec as P

SWEEPS = 2
highest = lax.Precision.HIGHEST


def with_halo(block, sides, width):
    for axis, dim in sides:
        count = lax.axis_size(axis)
        forward = [(i, i + 1) for i in range(count - 1)]
        backward = [(target, source) for source, target in forward]
        low = lax.ppermute(
            lax.slice_in_dim(block, block.shape[dim] - width, None, axis=dim), axis, forward
        )
        high = lax.ppermute(lax.slice_in_dim(block, 0, width, axis=dim), axis, backward)
        block = jnp.concatenate([low, block, high], axis=dim)
    return block


def shards(loads, diagonal, stiffness, neighbors, slot_mask, send_list, aggregate, coarse_inverse):
    ghost_rows = send_list.shape[0] // 2
    live_slots = slot_mask.astype(jnp.float32)
    diag_rows = diagonal[:, None, :]

    def operate(vector):
        outgoing = jnp.take(vector, send_list, axis=0)
        padded = with_halo(outgoing, (("wide", 0),), ghost_rows)
        extended = jnp.concatenate([vector, padded[:ghost_rows], padded[3 * ghost_rows :]], axis=0)
        gathered = jnp.take(extended, neighbors, axis=0) * live_slots[:, :, None, None]
        coupled = jnp.einsum("bscj,bsij->bci", gathered, stiffness, precision=highest)
        return diag_rows * vector - coupled

    scaled = loads / diag_rows
    row_sums = jnp.sum(jnp.sum(jnp.abs(stiffness), axis=3) * live_slots[:, :, None], axis=1)
    local_peak = jnp.max(row_sums / diagonal)
    upper_bound = 1.0 + lax.pmax(local_peak, ("wide", "narrow"))
    centre = 0.625 * upper_bound
    direction = scaled / centre
    applied = operate(direction)
    half_span = 0.375 * upper_bound
    spread_ratio = 5.0 / 3.0
    weight_prev = 0.6
    solution = direction
    remainder = loads
    for sweep_index in range(SWEEPS):
        if sweep_index > 0:
            applied = operate(direction)
        remainder = remainder - applied
        weight_now = 1.0 / (2.0 * spread_ratio - weight_prev)
        direction = (
            weight_now * weight_prev * direction
            + 2.0 * weight_now / half_span * remainder / diag_rows
        )
        solution = solution + direction
        weight_prev = weight_now
    residual = remainder - operate(direction)
    agg_cols = coarse_inverse.shape[0] * lax.axis_size("narrow")
    one_hot = (
        aggregate[:, :, None] == jnp.arange(agg_cols, dtype=jnp.int32)[None, None, :]
    ).astype(jnp.float32)
    part_sums = jnp.einsum("bci,big->cg", residual, one_hot, precision=highest)
    owned_sums = lax.psum_scatter(part_sums, "narrow", scatter_dimension=1, tiled=True)
    coarse_own = jnp.einsum(
        "ch,kh->ck",
        lax.all_gather(owned_sums, ("wide", "narrow"), axis=1, tiled=True),
        coarse_inverse,
        precision=highest,
    )
    coarse_group = lax.all_gather(coarse_own, "narrow", axis=1, tiled=True)
    spread_back = jnp.einsum("cg,big->bci", coarse_group, one_hot, precision=highest)
    return (solution + spread_back, residual)


def solution(mesh):
    return jax.shard_map(
        shards,
        mesh=mesh,
        in_specs=(
            P(("wide", "narrow"), None, None),
            P(("wide", "narrow"), None),
            P(("wide", "narrow"), None, None, None),
            P(("wide", "narrow"), None),
            P(("wide", "narrow"), None),
            P(("wide", "narrow")),
            P(("wide", "narrow"), None),
            P(("wide", "narrow"), None),
        ),
        out_specs=(P(("wide", "narrow"), None, None), P(("wide", "narrow"), None, None)),
        check_vma=False,
    )
```

profile of v0, /device:TPU:8, one launch (start us, length us, event | category | flops | bytes accessed | tf_op | source)
XLA Modules:
  0.0 1646.6 jit_solution(16821099746210735129)
XLA Ops:
  7.3 0.8 compare_and_fusion.1
  9.4 1.6 abs_reduce_fusion
  11.0 1.3 divide_reduce_fusion
  12.3 104.9 %pmax.7 = f32[]{:T(128)} all-reduce(f32[]{:T(128)} %divide_reduce_fusion), channel_id=1, replica_groups=mesh['wide'=64,'narrow'=8] {'wide','narrow'}, use_global_device_ids=true, to_apply=%region_3.0 | all-reduce | flops 1 | bytes 8 | tf_op jit(solution)/shard_map/pmax | solution.py:39
  117.9 0.7 broadcast_multiply_fusion
  118.5 0.8 broadcast_divide_fusion
  120.0 1.9 collective-permute-start
  121.9 6.3 collective-permute-start.1
  128.3 0.7 compare_and_fusion
  130.4 2.3 divide_add_fusion.1
  133.3 1.9 collective-permute-start.2
  135.2 6.3 collective-permute-start.3
  141.6 1.4 collective-permute-done.3
  143.7 1.0 divide_add_fusion
  145.4 1.9 collective-permute-start.4
  147.3 6.3 collective-permute-start.5
  153.7 1.5 collective-permute-done.5
  155.7 1.0 fusion.6
  156.8 1.1 convolution_bitcast_fusion
  157.9 87.4 %reduce-scatter.4.cloned.1.call-done = f32[16,24]{1,0:T(8,128)} async-done(((f32[128,24]{1,0:T(8,128)}), f32[16,24]{1,0:T(8,128)}) %reduce-scatter.4.cloned.1.call-update) | async-done | bytes 1552
  245.3 1344.6 %all_gather.6 = f32[24,8192]{0,1:T(8,128)S(1)} all-gather(f32[24,16]{0,1:T(8,128)} %bitcast.46), channel_id=1, replica_groups=mesh['wide'=64,'narrow'=8] {'wide','narrow'}, dimensions={1}, use_global_device_ids=true | all-gather | bytes 787968 | tf_op jit(solution)/shard_map/all_gather | solution.py:68
  1590.0 2.4 fusion.25
  1592.4 46.4 %all_gather.7 = f32[24,128]{0,1:T(8,128)S(1)} all-gather(f32[24,16]{0,1:T(8,128)S(1)} %fusion.25), channel_id=1, replica_groups=mesh['wide'=64,'narrow'=8] {'narrow'}, dimensions={1}, use_global_device_ids=true | all-gather | bytes 13824 | tf_op jit(solution)/shard_map/all_gather | solution.py:72
  1638.7 1.0 fusion
  (40 shorter events, 5.9 us)
Async XLA Ops:
  7.2 1582.8 %copy-start = (f32[16,8192]{1,0:T(8,128)S(1)}, f32[16,8192]{1,0:T(8,128)}, u32[]{:S(2)}) copy-start(f32[16,8192]{1,0:T(8,128)} %param.19) | copy-start | bytes 1572868
  7.2 136.5 %copy-start.1 = (f32[4,4,128,128]{3,2,1,0:T(8,128)S(1)}, f32[4,4,128,128]{3,2,1,0:T(8,128)}, u32[]{:S(2)}) copy-start(f32[4,4,128,128]{3,2,1,0:T(8,128)} %param.14) | copy-start | bytes 3145732
  7.2 136.5 %copy-start.3 = (f32[4,128]{1,0:T(4,128)S(1)}, f32[4,128]{1,0:T(4,128)}, u32[]{:S(2)}) copy-start(f32[4,128]{1,0:T(4,128)} %param.13) | copy-start | bytes 6148
  7.2 149.5 %copy-start.5 = (s32[4,128]{1,0:T(4,128)S(1)}, s32[4,128]{1,0:T(4,128)}, u32[]{:S(2)}) copy-start(s32[4,128]{1,0:T(4,128)} %param.18) | copy-start | bytes 6148
  7.2 238.1 %reduce-scatter.4.cloned.1.call-start = ((), (), s32[]{:S(2)}) async-start(), calls=%async_computation.1 | async-start | bytes 73728
  120.0 9.8 collective-permute-start
  121.9 7.9 collective-permute-start.1
  133.3 8.3 collective-permute-start.2
  135.2 7.8 collective-permute-start.3
  145.4 8.3 collective-permute-start.4
  147.3 7.8 collective-permute-start.5
  156.7 1435.6 %copy-start.4 = (f32[4,24,128]{2,1,0:T(8,128)}, f32[4,24,128]{2,1,0:T(8,128)S(1)}, u32[]{:S(2)}) copy-start(f32[4,24,128]{2,1,0:T(8,128)S(1)} %fusion.6) | copy-start | bytes 147460
  245.3 1393.4 %copy-start.2 = (f32[4,24,128]{2,1,0:T(8,128)S(1)}, f32[4,24,128]{2,1,0:T(8,128)}, u32[]{:S(2)}) copy-start(f32[4,24,128]{2,1,0:T(8,128)} %param.12) | copy-start | bytes 147460
Sparse Core Ops, SparseCore 0:
  158.0 87.2 reduce-scatter.3
where the time goes:
time: 1650 us
  blocking collectives  1500 us (91%)
  waiting for transfers between devices  90.4 us (5%)
  starting transfers between devices  24.8 us (2%)
    all_gather x1, blocking collectives, shards(): lax.all_gather(owned_sums, ('wide', 'narrow'), axis=1, tiled=True)  1340 us
    pmax x1, blocking collectives, shards(): upper_bound = 1.0 + lax.pmax(local_peak, ('wide', 'narrow'))  105 us
    unnamed x2, waiting for transfers between devices  87.4 us
    all_gather x1, blocking collectives, shards(): coarse_group = lax.all_gather(coarse_own, 'narrow', axis=1, tiled=True)  46.4 us
  transfers between devices with their start and end apart: 7, of which 3 were waited for; matrix products, arithmetic and copies ran while one was open for 0% of the time, Pallas kernels for 0%

commit v1 on v0

--- a/solution.py
+++ b/solution.py
@@ -69,7 +69,9 @@
         coarse_inverse,
         precision=highest,
     )
-    coarse_group = lax.all_gather(coarse_own, "narrow", axis=1, tiled=True)
+    coarse_group = jnp.concatenate(
+        lax.all_to_all(jnp.stack([coarse_own] * lax.axis_size("narrow")), "narrow", 0, 0), axis=1
+    )
     spread_back = jnp.einsum("cg,big->bci", coarse_group, one_hot, precision=highest)
     return (solution + spread_back, residual)
 

time: 1650 us -> 1620 us (0.982)
  the two profiles are of different devices: /device:TPU:8 before, /device:TPU:32 now
where the time goes in v1:
time: 1620 us
  blocking collectives  1470 us (91%)
  waiting for transfers between devices  88 us (5%)
  starting transfers between devices  28.4 us (2%)
    all_gather x1, blocking collectives, shards(): lax.all_gather(owned_sums, ('wide', 'narrow'), axis=1, tiled=True)  1350 us
    pmax x1, blocking collectives, shards(): upper_bound = 1.0 + lax.pmax(local_peak, ('wide', 'narrow'))  103 us
    unnamed x2, waiting for transfers between devices  85.1 us
  transfers between devices with their start and end apart: 7, of which 3 were waited for; matrix products, arithmetic and copies ran while one was open for 0% of the time, Pallas kernels for 0%

profile of v1, /device:TPU:32, one launch (start us, length us, event | category | flops | bytes accessed | tf_op | source)
XLA Modules:
  0.0 1622.2 jit_solution(11339732329270046076)
XLA Ops:
  7.3 0.8 convert_element_type.4
  8.0 1.6 abs_reduce_fusion
  10.4 1.3 divide_reduce_fusion
  12.3 103.4 %pmax.7 = f32[]{:T(128)} all-reduce(f32[]{:T(128)} %divide_reduce_fusion), channel_id=1, replica_groups=mesh['wide'=64,'narrow'=8] {'wide','narrow'}, use_global_device_ids=true, to_apply=%region_3.0 | all-reduce | flops 1 | bytes 8 | tf_op jit(solution)/shard_map/pmax | solution.py:39
  117.0 0.8 broadcast_divide_fusion
  118.5 1.9 collective-permute-start
  120.4 7.5 collective-permute-start.1
  128.0 0.7 compare_select_fusion
  128.7 0.7 compare_and_fusion
  130.1 2.3 divide_add_fusion.1
  133.0 1.9 collective-permute-start.2
  134.9 7.5 collective-permute-start.3
  142.6 1.4 collective-permute-done.3
  144.6 1.0 divide_add_fusion
  146.3 1.9 collective-permute-start.4
  148.2 7.6 collective-permute-start.5
  155.8 1.5 collective-permute-done.5
  157.8 1.0 fusion.6
  158.9 1.1 convolution_bitcast_fusion
  160.0 85.0 %reduce-scatter.4.cloned.1.call-done = f32[16,24]{1,0:T(8,128)} async-done(((f32[128,24]{1,0:T(8,128)}), f32[16,24]{1,0:T(8,128)}) %reduce-scatter.4.cloned.1.call-update) | async-done | bytes 1552
  245.1 1346.1 %all_gather.3 = f32[24,8192]{0,1:T(8,128)S(1)} all-gather(f32[24,16]{0,1:T(8,128)} %bitcast.54), channel_id=1, replica_groups=mesh['wide'=64,'narrow'=8] {'wide','narrow'}, dimensions={1}, use_global_device_ids=true | all-gather | bytes 787968 | tf_op jit(solution)/shard_map/all_gather | solution.py:68
  1591.1 2.4 fusion.24
  1593.7 19.4 %all_to_all.5 = f32[8,1,384]{2,1,0:T(1,128)S(1)} all-to-all(f32[8,1,384]{2,1,0:T(1,128)S(1)} %reshape.110), channel_id=1, replica_groups=mesh['wide'=64,'narrow'=8] {'narrow'}, dimensions={0} | all-to-all | bytes 24576 | tf_op jit(solution)/shard_map/all_to_all | solution.py:73
  1614.4 1.0 fusion
  (45 shorter events, 7.3 us)
Async XLA Ops:
  7.2 1584.0 %copy-start = (f32[16,8192]{1,0:T(8,128)S(1)}, f32[16,8192]{1,0:T(8,128)}, u32[]{:S(2)}) copy-start(f32[16,8192]{1,0:T(8,128)} %param.19) | copy-start | bytes 1572868
  7.2 137.4 %copy-start.1 = (f32[4,4,128,128]{3,2,1,0:T(8,128)S(1)}, f32[4,4,128,128]{3,2,1,0:T(8,128)}, u32[]{:S(2)}) copy-start(f32[4,4,128,128]{3,2,1,0:T(8,128)} %param.14) | copy-start | bytes 3145732
  7.2 137.4 %copy-start.3 = (f32[4,128]{1,0:T(4,128)S(1)}, f32[4,128]{1,0:T(4,128)}, u32[]{:S(2)}) copy-start(f32[4,128]{1,0:T(4,128)} %param.13) | copy-start | bytes 6148
  7.2 151.6 %copy-start.5 = (s32[4,128]{1,0:T(4,128)S(1)}, s32[4,128]{1,0:T(4,128)}, u32[]{:S(2)}) copy-start(s32[4,128]{1,0:T(4,128)} %param.18) | copy-start | bytes 6148
  7.2 237.8 %reduce-scatter.4.cloned.1.call-start = ((), (), s32[]{:S(2)}) async-start(), calls=%async_computation.2 | async-start | bytes 73728
  118.5 11.0 collective-permute-start
  120.4 9.1 collective-permute-start.1
  133.0 9.5 collective-permute-start.2
  134.9 9.1 collective-permute-start.3
  146.3 9.5 collective-permute-start.4
  148.2 9.1 collective-permute-start.5
  158.9 1434.7 %copy-start.4 = (f32[4,24,128]{2,1,0:T(8,128)}, f32[4,24,128]{2,1,0:T(8,128)S(1)}, u32[]{:S(2)}) copy-start(f32[4,24,128]{2,1,0:T(8,128)S(1)} %fusion.6) | copy-start | bytes 147460
  245.1 1369.3 %copy-start.2 = (f32[4,24,128]{2,1,0:T(8,128)S(1)}, f32[4,24,128]{2,1,0:T(8,128)}, u32[]{:S(2)}) copy-start(f32[4,24,128]{2,1,0:T(8,128)} %param.12) | copy-start | bytes 147460
Sparse Core Ops, SparseCore 0:
  160.1 84.8 reduce-scatter.3
